TPU v7x, 32 devices: a whole 2x2x4 slice. The times are simulated.
32 devices in a mesh: edge: 8 (over z, y), mp: 4 (over x, core).
Axes of the slice: x: 2, y: 2, z: 4, core: 2. Of those that a mesh axis runs over, the one named last changes fastest.
Arguments:
- edge_feat: bfloat16 [16384, 512], P('edge', 'mp'), may hold values from -6 to 6
- mirror_rows: int32 [16384], P('edge'), may hold values from 0 to 2047, as said below
- edge_slot: int32 [128, 128], P('edge'), may hold values from 0 to 15
- group_owner: int32 [512, 1], P('edge'), may hold values from 0 to 7; in each aligned block of 64 rows (0 to 63, 64 to 127, ...) at most 16 rows name the same one
- group_window: int32 [512], P('edge'), may hold values from 0 to 127
- up_edge: bfloat16 [512, 512], P(None, 'mp'), may hold values from -0.25 to 0.25
- down_edge: bfloat16 [512, 512], P('mp'), may hold values from -0.25 to 0.25
- mix_self: bfloat16 [512, 512], P(None, 'mp'), may hold values from -0.1875 to 0.1875
- mix_mirror: bfloat16 [512, 512], P(None, 'mp'), may hold values from -0.1875 to 0.1875
- up_atom: bfloat16 [512, 512], P(None, 'mp'), may hold values from -0.25 to 0.25
- down_atom: bfloat16 [512, 512], P('mp'), may hold values from -0.25 to 0.25
- atom_gain: float32 [512], replicated, may hold values from 0.1 to 1.9
Outputs:
- atom_out: bfloat16 [16384, 512], P('edge', 'mp')
Inputs may be any that keep to these rules, and one draw needn't show every extreme that they name: Within each block of 2048 rows mirror_rows is a permutation; the partner block holds its inverse permutation, so the matching of reverse edges is symmetric. `group_owner`: among the 64 groups of one device, no owner is named more than 16 times, and in every draw some device names some owner exactly 16 times.
All inputs are finite; a program needn't handle non-finite values.
Results may differ from a plain program's by a relative error of at most 0.014.
Values may be sent and summed in bfloat16 or wider, within the bound.
A program may use at most 64 MiB of HBM per device.

v0:
```python
import functools
import jax
import jax.numpy as jnp
from jax import lax
from jax.experimental import pallas as pl
from jax.experimental.pallas import tpu as pltpu
from jax.sharding import PartitionSpec as P

AW = 16
MESH = pl.DeviceIdType.MESH
F32 = jnp.float32
BF16 = jnp.bfloat16


def iota(shape, dim):
    return lax.broadcasted_iota(jnp.int32, shape, dim)


def one_hot(mask):
    return jnp.where(mask, 1.0, 0.0).astype(BF16)


def dot(a, b):
    return jnp.dot(a, b, preferred_element_type=F32)


def silu(v):
    return v / (1.0 + jnp.exp(-v))


def at(start, size):
    return pl.ds(pl.multiple_of(start, size), size)


def kernel(
    E, M, cap,
    x_in, mirror_in, slot_in, owner_in, window_in,
    up_e, down_e, mix_s, mix_m, up_a, down_a, gain_in,
    out,
    x, mirror, slot, owner_r, window_r, gain,
    perm, own, rev, g_up_e, g_down_e, g_mix_s, g_mix_m, g_up_a, g_down_a,
    one, mixed_self, part, part_cols, idx_send, idx_got, block_send, block_got,
    atom_cols, atom_rows, updated,
    own_s, own_r, rev_s, rev_r, w_s, w_r, idx_s, idx_r, part_s, part_r,
    block_s, block_r, atom_s, atom_r, out_s, out_r, local_w, local, load,
):
    R, W = x.shape
    Q, D = R // M, W * M
    CH = slot.shape[1]
    NC = Q // CH
    G = owner_r.shape[1]
    GR = R // G
    PR = CH // GR * AW
    NP = NC * PR
    PF = M * NP
    SR = cap * AW
    half = Q // 2
    e, m = lax.axis_index("edge"), lax.axis_index("mp")
    p = e ^ (E // 2)
    peers = sorted(range(1, M), reverse=True)

    def remote(src, dst, ss, rs, f, j):
        return pltpu.make_async_remote_copy(
            src_ref=src, dst_ref=dst, send_sem=ss, recv_sem=rs,
            device_id=(f, j), device_id_type=MESH,
        )

    loads = [
        pltpu.make_async_copy(src, dst, load.at[i])
        for i, (src, dst) in enumerate(
            [
                (mirror_in, mirror), (x_in, x), (owner_in, owner_r),
                (window_in, window_r), (slot_in, slot), (gain_in, gain),
            ]
        )
    ]
    for copy in loads:
        copy.start()

    barrier = pltpu.get_barrier_semaphore()
    for d in peers:
        pl.semaphore_signal(barrier, inc=1, device_id=(p, m ^ d), device_id_type=MESH)
        pl.semaphore_signal(barrier, inc=1, device_id=(e, m ^ d), device_id_type=MESH)

    def greet(d, _):
        pl.semaphore_signal(barrier, inc=1, device_id=(e ^ d, m), device_id_type=MESH)
        return 0

    lax.fori_loop(1, E, greet, 0)

    shards = (up_e, down_e, mix_s, mix_m, up_a, down_a)
    wholes = (g_up_e, g_down_e, g_mix_s, g_mix_m, g_up_a, g_down_a)
    by_rows = (False, True, False, False, False, True)
    bits = [1 << b for b in reversed(range(M.bit_length() - 1))]

    def low_bits(d):
        return [b for b in bits if d == 0 or b < (d & -d)]

    def shard_at(k, i):
        if by_rows[k]:
            return wholes[k].at[at(i * W, W), :]
        return wholes[k].at[:, at(i * W, W)]

    def w_copy(k, d, b):
        src = shards[k] if d == 0 else shard_at(k, m ^ d)
        return remote(src, shard_at(k, m ^ d), w_s.at[k, d, b], w_r.at[k, d ^ b], e, m ^ b)

    def w_own(k):
        return pltpu.make_async_copy(shards[k], shard_at(k, m), local_w.at[k])

    def w_start(k):
        for b in low_bits(0):
            w_copy(k, 0, b).start()

    def w_recv(k, d):
        b = d & -d
        w_copy(k, d ^ b, b).wait_recv()

    def w_finish(k):
        for d in sorted(range(1, M), key=lambda v: -(v & -v)):
            if low_bits(d):
                w_recv(k, d)
                for b in low_bits(d):
                    w_copy(k, d, b).start()

    def w_wait(k):
        w_own(k).wait()
        for d in range(1, M):
            if not low_bits(d):
                w_recv(k, d)

    def w_drain(k):
        for d in range(M):
            for b in low_bits(d):
                w_copy(k, d, b).wait_send()

    for k in range(6):
        w_own(k).start()

    def own_local():
        return pltpu.make_async_copy(x_in.at[at(m * Q, Q), :], own.at[:, at(m * W, W)], local.at[0])

    def own_copy(d):
        return remote(
            x_in.at[at((m ^ d) * Q, Q), :], own.at[:, at(m * W, W)],
            own_s.at[d], own_r.at[d], e, m ^ d,
        )

    own_local().start()

    def rev_build(c):
        for j in range(M):
            rows = j * Q + c * CH
            picks = one_hot(iota((CH, R), 0) + rows == mirror[...])
            perm[at(rows, CH), :] = dot(picks, x[...]).astype(BF16)

    def rev_copy(c, d):
        j = m ^ d
        return remote(
            perm.at[at(j * Q + c * CH, CH), :], rev.at[at(c * CH, CH), at(m * W, W)],
            rev_s.at[d, c], rev_r.at[d, c], p, j,
        )

    def rev_start(c):
        for d in [0] + peers[::-1]:
            rev_copy(c, d).start()

    for copy in loads:
        copy.wait()

    diag = iota((G, G), 0) == iota((G, G), 1)
    owner_c = jnp.sum(jnp.where(diag, owner_r[...], 0), axis=1, keepdims=True)
    k_g = lax.div(iota((G, G * AW), 1), AW)
    row_g = iota((G, G * AW), 0)
    owner_k = jnp.sum(jnp.where(k_g == row_g, owner_c, 0), axis=0, keepdims=True)
    rank_k = jnp.sum(
        jnp.where((owner_c == owner_k) & (row_g < k_g), 1, 0), axis=0, keepdims=True
    )
    target = (owner_k * cap + rank_k) * AW + lax.rem(iota((1, G * AW), 1), AW)
    window_c = jnp.sum(jnp.where(diag, window_r[...], 0), axis=1, keepdims=True)
    rank_c = jnp.sum(
        jnp.where((owner_c == owner_r[...]) & (iota((G, G), 1) < iota((G, G), 0)), 1, 0),
        axis=1, keepdims=True,
    )
    place_c = owner_c * cap + rank_c

    def atom_index(f):
        lane = iota((G, SR), 1)
        hit = place_c == f * cap + lax.div(lane, AW)
        value = jnp.sum(
            jnp.where(hit, window_c * AW + lax.rem(lane, AW) + 1, 0), axis=0, keepdims=True
        )
        return jnp.broadcast_to(value - 1, (8, SR))

    def idx_build(d, _):
        idx_send[e ^ d] = atom_index(e ^ d)
        return 0

    lax.fori_loop(1, E, idx_build, 0)
    idx_got[e] = atom_index(e)
    rev_build(0)

    pl.semaphore_wait(barrier, E - 1 + 2 * (M - 1))

    rev_start(0)
    for d in peers:
        own_copy(d).start()
    w_start(0)
    w_start(1)

    def rev_step(c, _):
        rev_build(c)
        rev_start(c)
        return 0

    lax.fori_loop(1, NC, rev_step, 0)
    w_start(2)
    w_start(3)

    def idx_copy(d):
        return remote(
            idx_send.at[e ^ d], idx_got.at[e], idx_s.at[d], idx_r.at[d], e ^ d, m
        )

    def idx_start(d, _):
        idx_copy(d).start()
        return 0

    lax.fori_loop(1, E, idx_start, 0)
    w_finish(0)
    w_finish(1)
    own_local().wait()
    for d in peers:
        own_copy(d).wait_recv()
    w_wait(0)
    w_wait(1)

    def edge_rows(rows):
        hidden = silu(dot(rows, g_up_e[...])).astype(BF16)
        return (rows.astype(F32) + dot(hidden, g_down_e[...])).astype(BF16)

    def own_step(i, _):
        one[at(i * half, half), :] = edge_rows(own[at(i * half, half), :])
        return 0

    lax.fori_loop(0, 2, own_step, 0)
    w_finish(2)
    w_wait(2)

    def self_step(i, _):
        mixed_self[at(i * half, half), :] = dot(one[at(i * half, half), :], g_mix_s[...])
        return 0

    lax.fori_loop(0, 2, self_step, 0)
    w_finish(3)
    w_wait(3)

    def part_copy(c, d):
        return remote(
            part.at[at(c * PR, PR), at((m ^ d) * W, W)],
            part_cols.at[at(m * NP + c * PR, PR), :],
            part_s.at[d, c], part_r.at[d, c], e, m ^ d,
        )

    def part_local(c):
        return pltpu.make_async_copy(
            part.at[at(c * PR, PR), at(m * W, W)],
            part_cols.at[at(m * NP + c * PR, PR), :], part_s.at[0, c],
        )

    def edge_step(c, _):
        for d in peers + [0]:
            rev_copy(c, d).wait_recv()
        rows = at(c * CH, CH)
        reverse = edge_rows(rev[rows, :])
        mixed = mixed_self[rows, :] + dot(reverse, g_mix_m[...])
        two = (one[rows, :].astype(F32) + silu(mixed)).astype(BF16)
        spot = lax.div(iota((PR, CH), 1), GR) * AW + slot[pl.ds(m * NC + c, 1), :]
        part[at(c * PR, PR), :] = dot(one_hot(iota((PR, CH), 0) == spot), two).astype(BF16)
        part_local(c).start()
        for d in peers:
            part_copy(c, d).start()
        return 0

    lax.fori_loop(0, NC, edge_step, 0)
    w_start(4)
    w_start(5)

    def part_wait(c, _):
        part_local(c).wait()
        for d in peers:
            part_copy(c, d).wait_recv()
        return 0

    lax.fori_loop(0, NC, part_wait, 0)

    def owner_block(f):
        return dot(one_hot(iota((SR, PF), 0) + f * SR == target), part_cols[...]).astype(BF16)

    def block_copy(d):
        return remote(
            block_send.at[e ^ d], block_got.at[e], block_s.at[d], block_r.at[d], e ^ d, m
        )

    def block_step(i, _):
        d = E - i
        block_send[e ^ d] = owner_block(e ^ d)
        block_copy(d).start()
        return 0

    lax.fori_loop(1, E, block_step, 0)
    block_got[e] = owner_block(e)
    w_finish(4)
    w_finish(5)

    def block_wait(d, _):
        idx_copy(d).wait_recv()
        block_copy(d).wait_recv()
        return 0

    lax.fori_loop(1, E, block_wait, 0)

    def atom_copy(h, d):
        return remote(
            atom_cols.at[at((m ^ d) * Q + h * half, half), :],
            atom_rows.at[at(h * half, half), at(m * W, W)],
            atom_s.at[d, h], atom_r.at[d, h], e, m ^ d,
        )

    def atom_local(h):
        return pltpu.make_async_copy(
            atom_cols.at[at(m * Q + h * half, half), :],
            atom_rows.at[at(h * half, half), at(m * W, W)], atom_s.at[0, h],
        )

    def placed(start):
        def add(f, total):
            picks = one_hot(iota((half, SR), 0) + start == idx_got[f][:1, :])
            return total + dot(picks, block_got[f])

        if E * SR > 8 * R:
            unroll = 1
        else:
            unroll = min(E, 8)
        return lax.fori_loop(0, E, add, jnp.zeros((half, W), F32), unroll=unroll)

    for h in range(2):
        for d in peers + [0]:
            start = (m ^ d) * Q + h * half
            atom_cols[at(start, half), :] = placed(start).astype(BF16)
            if d:
                atom_copy(h, d).start()
            else:
                atom_local(h).start()

    w_wait(4)
    w_wait(5)

    def out_copy(c, d):
        return remote(
            updated.at[at(c * half, half), at((m ^ d) * W, W)],
            out.at[at(m * Q + c * half, half), :],
            out_s.at[d, c], out_r.at[d, c], e, m ^ d,
        )

    def out_local(c):
        return pltpu.make_async_copy(
            updated.at[at(c * half, half), at(m * W, W)],
            out.at[at(m * Q + c * half, half), :], out_s.at[0, c],
        )

    def atom_step(c, _):
        rows = at(c * half, half)
        atom_local(c).wait()
        for d in peers:
            atom_copy(c, d).wait_recv()
        atoms = atom_rows[rows, :].astype(F32)
        scale = lax.rsqrt(jnp.sum(atoms * atoms, axis=1, keepdims=True) / D + 1e-06)
        normed = (atoms * scale * gain[...]).astype(BF16)
        hidden = silu(dot(normed, g_up_a[...])).astype(BF16)
        updated[rows, :] = (atoms + dot(hidden, g_down_a[...])).astype(BF16)
        for d in peers:
            out_copy(c, d).start()
        out_local(c).start()
        return 0

    lax.fori_loop(0, 2, atom_step, 0)

    for d in peers:
        own_copy(d).wait_send()
        for h in range(2):
            atom_copy(h, d).wait_send()
    for k in range(6):
        w_drain(k)

    def drain_chunk(c, _):
        for d in peers + [0]:
            rev_copy(c, d).wait_send()
        for d in peers:
            part_copy(c, d).wait_send()
        return 0

    lax.fori_loop(0, NC, drain_chunk, 0)

    def drain_owner(d, _):
        idx_copy(d).wait_send()
        block_copy(d).wait_send()
        return 0

    lax.fori_loop(1, E, drain_owner, 0)
    for c in range(2):
        out_local(c).wait()
        for d in peers:
            out_copy(c, d).wait_send()
            out_copy(c, d).wait_recv()


def body(E, M, x, mirror, slot, owner, window, up_e, down_e, mix_s, mix_m, up_a, down_a, gain):
    R, W = x.shape
    Q, D = R // M, W * M
    NC = Q // slot.shape[1]
    G = owner.shape[0]
    anywhere = pl.BlockSpec(memory_space=pl.ANY)
    cap = max(2, 2 * G // E)
    SR = cap * AW
    NP = Q // (R // G) * AW
    vmem = pl.BlockSpec(memory_space=pl.ANY)
    dma = pltpu.SemaphoreType.DMA
    return pl.pallas_call(
        functools.partial(kernel, E, M, cap),
        name="edge_window",
        out_shape=jax.ShapeDtypeStruct((R, W), BF16),
        in_specs=[anywhere] * 12,
        out_specs=vmem,
        scratch_shapes=[
            pltpu.VMEM((R, W), BF16),
            pltpu.VMEM((1, R), jnp.int32),
            pltpu.VMEM(slot.shape, jnp.int32),
            pltpu.VMEM((1, G), jnp.int32),
            pltpu.VMEM((1, G), jnp.int32),
            pltpu.VMEM((1, D), F32),
            pltpu.VMEM((R, W), BF16),
            pltpu.VMEM((Q, D), BF16),
            pltpu.VMEM((Q, D), BF16),
        ]
        + [pltpu.VMEM((D, D), BF16)] * 6
        + [
            pltpu.VMEM((Q, D), BF16),
            pltpu.VMEM((Q, D), F32),
            pltpu.VMEM((NP, D), BF16),
            pltpu.VMEM((M * NP, W), BF16),
            pltpu.VMEM((E, 8, SR), jnp.int32),
            pltpu.VMEM((E, 8, SR), jnp.int32),
            pltpu.VMEM((E, SR, W), BF16),
            pltpu.VMEM((E, SR, W), BF16),
            pltpu.VMEM((R, W), BF16),
            pltpu.VMEM((Q, D), BF16),
            pltpu.VMEM((Q, D), BF16),
            dma((M,)), dma((M,)),
            dma((M, NC)), dma((M, NC)),
            dma((6, M, M)), dma((6, M)),
            dma((E,)), dma((E,)),
            dma((M, NC)), dma((M, NC)),
            dma((E,)), dma((E,)),
            dma((M, 2)), dma((M, 2)),
            dma((M, 2)), dma((M, 2)),
            dma((6,)), dma((2,)), dma((6,)),
        ],
        compiler_params=pltpu.CompilerParams(collective_id=0, has_side_effects=True),
    )(
        x, mirror.reshape(1, R), slot, owner.reshape(1, G), window.reshape(1, G),
        up_e, down_e, mix_s, mix_m, up_a, down_a, gain.reshape(1, D),
    )


def solution(mesh):
    E, M = mesh.shape["edge"], mesh.shape["mp"]
    in_specs = (
        P("edge", "mp"),
        P("edge"),
        P("edge", None),
        P("edge", None),
        P("edge"),
        P(None, "mp"),
        P("mp", None),
        P(None, "mp"),
        P(None, "mp"),
        P(None, "mp"),
        P("mp", None),
        P(),
    )
    return jax.shard_map(
        functools.partial(body, E, M),
        mesh=mesh, in_specs=in_specs, out_specs=P("edge", "mp"), check_vma=False,
    )
```

profile of v0, /device:TPU:0, one launch (start us, length us, event | category | flops | bytes accessed | tf_op | source)
XLA Modules:
  0.0 67.8 jit_solution(6485130447250079504)
XLA Ops:
  0.0 65.9 %edge_window.1 = bf16[2048,128]{1,0:T(8,128)(2,1)} custom-call(bf16[2048,128]{1,0:T(8,128)(2,1)} %x_in.1, s32[1,2048]{1,0:T(1,128)} %bitcast.4, s32[16,128]{1,0:T(8,128)} %slot_in.1, s32[1,64]{1,0:T(1,128)} %bitcast.6, s32[1,64]{1,0:T(1,128)} %bitcast.7, bf16[512,128]{1,0:T(8,128)(2,1)} %up_e.1, bf16[128,512]{1,0:T(8,128)(2,1)} %down_e.1, ...), custom_call_target="tpu_custom_call" | custom-call | tf_op jit(solution)/shard_map/edge_window/pallas_call | solution.py:429
  65.9 1.9 %copy.14 = bf16[2048,128]{1,0:T(8,128)(2,1)} copy(bf16[2048,128]{1,0:T(8,128)(2,1)} %edge_window.1) | data formatting | bytes 1048576
where the time goes:
time: 68 us; the launch traced here: 67.8 us
  Pallas kernels  65.9 us (97%)
  local copies, waits for them, and re-layouts  1.87 us (3%)
    pallas_call x1, Pallas kernels, body(): pl.pallas_call(functools.partial(kernel, E, M, cap), name='edge_window',...  65.9 us
    unnamed x1, local copies, waits for them, and re-layouts  1.87 us

commit v1 on v0

--- a/solution.py
+++ b/solution.py
@@ -39,10 +39,10 @@
     out,
     x, mirror, slot, owner_r, window_r, gain,
     perm, own, rev, g_up_e, g_down_e, g_mix_s, g_mix_m, g_up_a, g_down_a,
-    one, mixed_self, part, part_cols, idx_send, idx_got, block_send, block_got,
-    atom_cols, atom_rows, updated,
+    one, mixed_self, part, part_cols, idx_send, idx_got, select, block_send, block_got,
+    total, atom_rows, updated,
     own_s, own_r, rev_s, rev_r, w_s, w_r, idx_s, idx_r, part_s, part_r,
-    block_s, block_r, atom_s, atom_r, out_s, out_r, local_w, local, load,
+    block_s, block_r, relay_s, relay_r, out_s, out_r, local_w, local, load,
 ):
     R, W = x.shape
     Q, D = R // M, W * M
@@ -55,8 +55,11 @@
     PF = M * NP
     SR = cap * AW
     half = Q // 2
+    RH = R // 2
+    AC = RH // half
     e, m = lax.axis_index("edge"), lax.axis_index("mp")
     p = e ^ (E // 2)
+    side, pair = m % 2, m // 2
     peers = sorted(range(1, M), reverse=True)
 
     def remote(src, dst, ss, rs, f, j):
@@ -96,43 +99,82 @@
     def low_bits(d):
         return [b for b in bits if d == 0 or b < (d & -d)]
 
+    high = [b for b in bits if b > 1]
+    even = sorted(range(2, M, 2), key=lambda v: -(v & -v))
+    mine, other = e % 2, 1 - e % 2
+
     def shard_at(k, i):
         if by_rows[k]:
             return wholes[k].at[at(i * W, W), :]
         return wholes[k].at[:, at(i * W, W)]
 
-    def w_copy(k, d, b):
-        src = shards[k] if d == 0 else shard_at(k, m ^ d)
-        return remote(src, shard_at(k, m ^ d), w_s.at[k, d, b], w_r.at[k, d ^ b], e, m ^ b)
+    def half_at(k, i, h):
+        if by_rows[k]:
+            return wholes[k].at[pl.ds(pl.multiple_of(i * W + h * (W // 2), W // 2), W // 2), :]
+        return wholes[k].at[at(h * (D // 2), D // 2), at(i * W, W)]
+
+    def w_near(k):
+        return remote(shards[k], shard_at(k, m), w_s.at[k, 0, 1], w_r.at[k, 1, 0], e, m ^ 1)
+
+    def w_far(k, d, b):
+        if d:
+            src = half_at(k, m ^ d, mine)
+        else:
+            rows = shards[k].shape[0] // 2
+            src = shards[k].at[at(mine * rows, rows), :]
+        return remote(
+            src, half_at(k, m ^ d, mine), w_s.at[k, d, b], w_r.at[k, d ^ b, 0], e, m ^ b
+        )
+
+    def w_swap(k, d):
+        ref = half_at(k, m ^ d, mine)
+        return remote(ref, ref, w_s.at[k, d, M], w_r.at[k, d, 1], e ^ 1, m)
+
+    def w_pass(k, d, j):
+        ref = half_at(k, m ^ d, other if j else mine)
+        return remote(ref, ref, w_s.at[k, d, M + 1 + j], w_r.at[k, d ^ 1, j], e, m ^ 1)
 
     def w_own(k):
         return pltpu.make_async_copy(shards[k], shard_at(k, m), local_w.at[k])
 
     def w_start(k):
-        for b in low_bits(0):
-            w_copy(k, 0, b).start()
-
-    def w_recv(k, d):
-        b = d & -d
-        w_copy(k, d ^ b, b).wait_recv()
+        for b in high:
+            w_far(k, 0, b).start()
+        w_near(k).start()
 
     def w_finish(k):
-        for d in sorted(range(1, M), key=lambda v: -(v & -v)):
-            if low_bits(d):
-                w_recv(k, d)
-                for b in low_bits(d):
-                    w_copy(k, d, b).start()
+        for d in even:
+            b = d & -d
+            w_far(k, d ^ b, b).wait_recv()
+            w_swap(k, d).start()
+            for c in high:
+                if c < b:
+                    w_far(k, d, c).start()
+            w_pass(k, d, 0).start()
+
+    def w_second(k):
+        for d in even:
+            w_swap(k, d).wait_recv()
+            w_pass(k, d, 1).start()
 
     def w_wait(k):
         w_own(k).wait()
-        for d in range(1, M):
-            if not low_bits(d):
-                w_recv(k, d)
+        w_near(k).wait_recv()
+        for d in even:
+            for j in range(2):
+                w_pass(k, d, j).wait_recv()
 
     def w_drain(k):
-        for d in range(M):
-            for b in low_bits(d):
-                w_copy(k, d, b).wait_send()
+        w_near(k).wait_send()
+        for b in high:
+            w_far(k, 0, b).wait_send()
+        for d in even:
+            w_swap(k, d).wait_send()
+            for c in high:
+                if c < (d & -d):
+                    w_far(k, d, c).wait_send()
+            for j in range(2):
+                w_pass(k, d, j).wait_send()
 
     for k in range(6):
         w_own(k).start()
@@ -205,17 +247,14 @@
     rev_start(0)
     for d in peers:
         own_copy(d).start()
-    w_start(0)
-    w_start(1)
-
-    def rev_step(c, _):
+    for c in range(1, NC):
         rev_build(c)
         rev_start(c)
-        return 0
-
-    lax.fori_loop(1, NC, rev_step, 0)
-    w_start(2)
-    w_start(3)
+        for k in (2 * c - 2, 2 * c - 1):
+            if k < 6:
+                w_start(k)
+    for k in range(max(0, 2 * NC - 2), 6):
+        w_start(k)
 
     def idx_copy(d):
         return remote(
@@ -227,11 +266,19 @@
         return 0
 
     lax.fori_loop(1, E, idx_start, 0)
+
+    def select_build(f, _):
+        select[at(f * SR, SR), :] = one_hot(iota((SR, PF), 0) + f * SR == target)
+        return 0
+
+    lax.fori_loop(0, E, select_build, 0)
     w_finish(0)
     w_finish(1)
     own_local().wait()
     for d in peers:
         own_copy(d).wait_recv()
+    w_second(0)
+    w_second(1)
     w_wait(0)
     w_wait(1)
 
@@ -245,6 +292,9 @@
 
     lax.fori_loop(0, 2, own_step, 0)
     w_finish(2)
+    w_finish(3)
+    w_second(2)
+    w_second(3)
     w_wait(2)
 
     def self_step(i, _):
@@ -252,7 +302,6 @@
         return 0
 
     lax.fori_loop(0, 2, self_step, 0)
-    w_finish(3)
     w_wait(3)
 
     def part_copy(c, d):
@@ -282,9 +331,12 @@
             part_copy(c, d).start()
         return 0
 
-    lax.fori_loop(0, NC, edge_step, 0)
-    w_start(4)
-    w_start(5)
+    lax.fori_loop(0, NC - 1, edge_step, 0)
+    w_finish(4)
+    w_finish(5)
+    w_second(4)
+    w_second(5)
+    edge_step(NC - 1, 0)
 
     def part_wait(c, _):
         part_local(c).wait()
@@ -295,101 +347,138 @@
     lax.fori_loop(0, NC, part_wait, 0)
 
     def owner_block(f):
-        return dot(one_hot(iota((SR, PF), 0) + f * SR == target), part_cols[...]).astype(BF16)
+        return dot(select[at(f * SR, SR), :], part_cols[...]).astype(BF16)
+
+    def block_at(f, i):
+        return block_got.at[at(f * SR, SR), at(i * W, W)]
 
     def block_copy(d):
         return remote(
-            block_send.at[e ^ d], block_got.at[e], block_s.at[d], block_r.at[d], e ^ d, m
-        )
-
-    def block_step(i, _):
-        d = E - i
+            block_send.at[e ^ d], block_at(e, m), block_s.at[d], block_r.at[d], e ^ d, m
+        )
+
+    def block_step(d, _):
         block_send[e ^ d] = owner_block(e ^ d)
         block_copy(d).start()
         return 0
 
     lax.fori_loop(1, E, block_step, 0)
-    block_got[e] = owner_block(e)
-    w_finish(4)
-    w_finish(5)
-
-    def block_wait(d, _):
+    block_got[at(e * SR, SR), at(m * W, W)] = owner_block(e)
+
+    hops = [(j, b) for j in range(M) for b in low_bits(j)]
+
+    def relay(d, j, b):
+        ref = block_at(e ^ d, m ^ j)
+        return remote(
+            ref, ref, relay_s.at[d, hops.index((j, b))], relay_r.at[d, j ^ b], e, m ^ b
+        )
+
+    def relay_first(d):
+        for b in low_bits(0):
+            relay(d, 0, b).start()
+
+    def relay_next(d):
+        for j in sorted(range(1, M), key=lambda v: -(v & -v)):
+            if low_bits(j):
+                b = j & -j
+                relay(d, j ^ b, b).wait_recv()
+                for c in low_bits(j):
+                    relay(d, j, c).start()
+
+    def relay_wait(d):
+        for j in range(1, M):
+            if not low_bits(j):
+                b = j & -j
+                relay(d, j ^ b, b).wait_recv()
+
+    def arrive(d):
         idx_copy(d).wait_recv()
         block_copy(d).wait_recv()
-        return 0
-
-    lax.fori_loop(1, E, block_wait, 0)
-
-    def atom_copy(h, d):
-        return remote(
-            atom_cols.at[at((m ^ d) * Q + h * half, half), :],
-            atom_rows.at[at(h * half, half), at(m * W, W)],
-            atom_s.at[d, h], atom_r.at[d, h], e, m ^ d,
-        )
-
-    def atom_local(h):
-        return pltpu.make_async_copy(
-            atom_cols.at[at(m * Q + h * half, half), :],
-            atom_rows.at[at(h * half, half), at(m * W, W)], atom_s.at[0, h],
-        )
-
-    def placed(start):
-        def add(f, total):
-            picks = one_hot(iota((half, SR), 0) + start == idx_got[f][:1, :])
-            return total + dot(picks, block_got[f])
-
-        if E * SR > 8 * R:
-            unroll = 1
-        else:
-            unroll = min(E, 8)
-        return lax.fori_loop(0, E, add, jnp.zeros((half, W), F32), unroll=unroll)
-
-    for h in range(2):
-        for d in peers + [0]:
-            start = (m ^ d) * Q + h * half
-            atom_cols[at(start, half), :] = placed(start).astype(BF16)
-            if d:
-                atom_copy(h, d).start()
-            else:
-                atom_local(h).start()
-
+        relay_first(d)
+
+    def placed(d, start):
+        f = e ^ d
+        picks = one_hot(iota((half, SR), 0) + start == idx_got[f][:1, :])
+        return dot(picks, block_got[at(f * SR, SR), :])
+
+    def gather(i):
+        relay_wait(2 * i)
+        relay_wait(2 * i + 1)
+
+    def add(i):
+        gather(i)
+
+        def add_rows(r, _):
+            start = side * RH + r * half
+            rows = at(r * half, half)
+            total[rows, :] += placed(2 * i, start) + placed(2 * i + 1, start)
+            return 0
+
+        lax.fori_loop(0, AC, add_rows, 0)
+
+    def clear(r, _):
+        total[at(r * half, half), :] = jnp.zeros((half, D), F32)
+        return 0
+
+    relay_first(0)
+    lax.fori_loop(0, AC, clear, 0)
+    arrive(1)
+    last = E // 2 - 1
+
+    def stage(i):
+        arrive(2 * i + 2)
+        arrive(2 * i + 3)
+        relay_next(2 * i)
+        relay_next(2 * i + 1)
+
+    def flow(i, _):
+        stage(i)
+        add(i - 1)
+        return 0
+
+    stage(0)
+    lax.fori_loop(1, last, flow, 0)
+    add(last - 1)
+    relay_next(2 * last)
+    relay_next(2 * last + 1)
     w_wait(4)
     w_wait(5)
-
-    def out_copy(c, d):
-        return remote(
-            updated.at[at(c * half, half), at((m ^ d) * W, W)],
-            out.at[at(m * Q + c * half, half), :],
-            out_s.at[d, c], out_r.at[d, c], e, m ^ d,
-        )
-
-    def out_local(c):
+    gather(last)
+
+    def out_rows(r, s):
+        return out.at[at(s * RH + r * half, half), :]
+
+    def out_copy(r):
+        return remote(
+            updated.at[at(r * half, half), at((1 - side) * W, W)], out_rows(r, side),
+            out_s.at[1, r], out_r.at[r], e, m ^ 1,
+        )
+
+    def out_local(r):
         return pltpu.make_async_copy(
-            updated.at[at(c * half, half), at(m * W, W)],
-            out.at[at(m * Q + c * half, half), :], out_s.at[0, c],
-        )
-
-    def atom_step(c, _):
-        rows = at(c * half, half)
-        atom_local(c).wait()
-        for d in peers:
-            atom_copy(c, d).wait_recv()
+            updated.at[at(r * half, half), at(side * W, W)], out_rows(r, side), out_s.at[0, r]
+        )
+
+    def atom_step(r, _):
+        rows = at(r * half, half)
+        start = side * RH + r * half
+        sums = total[rows, :] + (placed(2 * last, start) + placed(2 * last + 1, start))
+        atom_rows[rows, :] = sums.astype(BF16)
         atoms = atom_rows[rows, :].astype(F32)
         scale = lax.rsqrt(jnp.sum(atoms * atoms, axis=1, keepdims=True) / D + 1e-06)
         normed = (atoms * scale * gain[...]).astype(BF16)
         hidden = silu(dot(normed, g_up_a[...])).astype(BF16)
-        updated[rows, :] = (atoms + dot(hidden, g_down_a[...])).astype(BF16)
-        for d in peers:
-            out_copy(c, d).start()
-        out_local(c).start()
-        return 0
-
-    lax.fori_loop(0, 2, atom_step, 0)
+        columns = at(pair * (2 * W), 2 * W)
+        kept = atom_rows[rows, columns].astype(F32)
+        updated[rows, :] = (kept + dot(hidden, g_down_a[:, columns])).astype(BF16)
+        out_copy(r).start()
+        out_local(r).start()
+        return 0
+
+    lax.fori_loop(0, AC, atom_step, 0)
 
     for d in peers:
         own_copy(d).wait_send()
-        for h in range(2):
-            atom_copy(h, d).wait_send()
     for k in range(6):
         w_drain(k)
 
@@ -402,17 +491,22 @@
 
     lax.fori_loop(0, NC, drain_chunk, 0)
 
+    def drain_relay(d):
+        for j, b in hops:
+            relay(d, j, b).wait_send()
+
     def drain_owner(d, _):
         idx_copy(d).wait_send()
         block_copy(d).wait_send()
-        return 0
-
+        drain_relay(d)
+        return 0
+
+    drain_relay(0)
     lax.fori_loop(1, E, drain_owner, 0)
-    for c in range(2):
-        out_local(c).wait()
-        for d in peers:
-            out_copy(c, d).wait_send()
-            out_copy(c, d).wait_recv()
+    for r in range(AC):
+        out_local(r).wait()
+        out_copy(r).wait_send()
+        out_copy(r).wait_recv()
 
 
 def body(E, M, x, mirror, slot, owner, window, up_e, down_e, mix_s, mix_m, up_a, down_a, gain):
@@ -424,6 +518,7 @@
     cap = max(2, 2 * G // E)
     SR = cap * AW
     NP = Q // (R // G) * AW
+    AC = R // 2 // (Q // 2)
     vmem = pl.BlockSpec(memory_space=pl.ANY)
     dma = pltpu.SemaphoreType.DMA
     return pl.pallas_call(
@@ -451,19 +546,20 @@
             pltpu.VMEM((M * NP, W), BF16),
             pltpu.VMEM((E, 8, SR), jnp.int32),
             pltpu.VMEM((E, 8, SR), jnp.int32),
+            pltpu.VMEM((E * SR, M * NP), BF16),
             pltpu.VMEM((E, SR, W), BF16),
-            pltpu.VMEM((E, SR, W), BF16),
-            pltpu.VMEM((R, W), BF16),
-            pltpu.VMEM((Q, D), BF16),
-            pltpu.VMEM((Q, D), BF16),
+            pltpu.VMEM((E * SR, D), BF16),
+            pltpu.VMEM((R // 2, D), F32),
+            pltpu.VMEM((R // 2, D), BF16),
+            pltpu.VMEM((R // 2, 2 * W), BF16),
             dma((M,)), dma((M,)),
             dma((M, NC)), dma((M, NC)),
-            dma((6, M, M)), dma((6, M)),
+            dma((6, M, M + 3)), dma((6, M, 2)),
             dma((E,)), dma((E,)),
             dma((M, NC)), dma((M, NC)),
             dma((E,)), dma((E,)),
-            dma((M, 2)), dma((M, 2)),
-            dma((M, 2)), dma((M, 2)),
+            dma((E, M - 1)), dma((E, M)),
+            dma((2, AC)), dma((AC,)),
             dma((6,)), dma((2,)), dma((6,)),
         ],
         compiler_params=pltpu.CompilerParams(collective_id=0, has_side_effects=True),

time: 68 us -> 75.8 us (1.11)
  Pallas kernels: 65.9 us -> 73.7 us
    pallas_call x1, Pallas kernels: 65.9 us -> 73.7 us  [body(): pl.pallas_call(functools.partial(kernel, E, M, cap), name='edge_window',...]
where the time goes in v1:
time: 75.8 us; the launch traced here: 75.6 us
  Pallas kernels  73.7 us (97%)
  local copies, waits for them, and re-layouts  1.87 us (2%)
    pallas_call x1, Pallas kernels, body(): pl.pallas_call(functools.partial(kernel, E, M, cap), name='edge_window',...  73.7 us
    unnamed x1, local copies, waits for them, and re-layouts  1.87 us

profile of v1, /device:TPU:0, one launch (start us, length us, event | category | flops | bytes accessed | tf_op | source)
XLA Modules:
  0.0 75.6 jit_solution(5454648909312904166)
XLA Ops:
  0.0 73.7 %edge_window.1 = bf16[2048,128]{1,0:T(8,128)(2,1)} custom-call(bf16[2048,128]{1,0:T(8,128)(2,1)} %x_in.1, s32[1,2048]{1,0:T(1,128)} %bitcast.4, s32[16,128]{1,0:T(8,128)} %slot_in.1, s32[1,64]{1,0:T(1,128)} %bitcast.6, s32[1,64]{1,0:T(1,128)} %bitcast.7, bf16[512,128]{1,0:T(8,128)(2,1)} %up_e.1, bf16[128,512]{1,0:T(8,128)(2,1)} %down_e.1, ...), custom_call_target="tpu_custom_call" | custom-call | tf_op jit(solution)/shard_map/edge_window/pallas_call | solution.py:524
  73.7 1.9 %copy.14 = bf16[2048,128]{1,0:T(8,128)(2,1)} copy(bf16[2048,128]{1,0:T(8,128)(2,1)} %edge_window.1) | data formatting | bytes 1048576

commit v2 on v1

--- a/solution.py
+++ b/solution.py
@@ -102,6 +102,7 @@
     high = [b for b in bits if b > 1]
     even = sorted(range(2, M, 2), key=lambda v: -(v & -v))
     mine, other = e % 2, 1 - e % 2
+    swapped = (0, 1, 2, 3)
 
     def shard_at(k, i):
         if by_rows[k]:
@@ -117,6 +118,11 @@
         return remote(shards[k], shard_at(k, m), w_s.at[k, 0, 1], w_r.at[k, 1, 0], e, m ^ 1)
 
     def w_far(k, d, b):
+        if k not in swapped:
+            src = shard_at(k, m ^ d) if d else shards[k]
+            return remote(
+                src, shard_at(k, m ^ d), w_s.at[k, d, b], w_r.at[k, d ^ b, 0], e, m ^ b
+            )
         if d:
             src = half_at(k, m ^ d, mine)
         else:
@@ -131,7 +137,10 @@
         return remote(ref, ref, w_s.at[k, d, M], w_r.at[k, d, 1], e ^ 1, m)
 
     def w_pass(k, d, j):
-        ref = half_at(k, m ^ d, other if j else mine)
+        if k not in swapped:
+            ref = shard_at(k, m ^ d)
+        else:
+            ref = half_at(k, m ^ d, other if j else mine)
         return remote(ref, ref, w_s.at[k, d, M + 1 + j], w_r.at[k, d ^ 1, j], e, m ^ 1)
 
     def w_own(k):
@@ -146,14 +155,15 @@
         for d in even:
             b = d & -d
             w_far(k, d ^ b, b).wait_recv()
-            w_swap(k, d).start()
+            if k in swapped:
+                w_swap(k, d).start()
             for c in high:
                 if c < b:
                     w_far(k, d, c).start()
             w_pass(k, d, 0).start()
 
     def w_second(k):
-        for d in even:
+        for d in even if k in swapped else ():
             w_swap(k, d).wait_recv()
             w_pass(k, d, 1).start()
 
@@ -161,7 +171,7 @@
         w_own(k).wait()
         w_near(k).wait_recv()
         for d in even:
-            for j in range(2):
+            for j in range(1 + (k in swapped)):
                 w_pass(k, d, j).wait_recv()
 
     def w_drain(k):
@@ -169,11 +179,12 @@
         for b in high:
             w_far(k, 0, b).wait_send()
         for d in even:
-            w_swap(k, d).wait_send()
+            if k in swapped:
+                w_swap(k, d).wait_send()
             for c in high:
                 if c < (d & -d):
                     w_far(k, d, c).wait_send()
-            for j in range(2):
+            for j in range(1 + (k in swapped)):
                 w_pass(k, d, j).wait_send()
 
     for k in range(6):
@@ -244,28 +255,26 @@
 
     pl.semaphore_wait(barrier, E - 1 + 2 * (M - 1))
 
+    def idx_copy(d):
+        return remote(
+            idx_send.at[e ^ d, pl.ds(0, 1), :], idx_got.at[e, pl.ds(0, 1), :], idx_s.at[d], idx_r.at[d], e ^ d, m
+        )
+
+    def idx_start(d, _):
+        idx_copy(d).start()
+        return 0
+
+    lax.fori_loop(1, E, idx_start, 0)
+
     rev_start(0)
     for d in peers:
         own_copy(d).start()
-    for c in range(1, NC):
+    w_start(0)
+    w_start(1)
+    rev_build(1)
+    rev_start(1)
+    for c in range(2, NC):
         rev_build(c)
-        rev_start(c)
-        for k in (2 * c - 2, 2 * c - 1):
-            if k < 6:
-                w_start(k)
-    for k in range(max(0, 2 * NC - 2), 6):
-        w_start(k)
-
-    def idx_copy(d):
-        return remote(
-            idx_send.at[e ^ d], idx_got.at[e], idx_s.at[d], idx_r.at[d], e ^ d, m
-        )
-
-    def idx_start(d, _):
-        idx_copy(d).start()
-        return 0
-
-    lax.fori_loop(1, E, idx_start, 0)
 
     def select_build(f, _):
         select[at(f * SR, SR), :] = one_hot(iota((SR, PF), 0) + f * SR == target)
@@ -274,6 +283,10 @@
     lax.fori_loop(0, E, select_build, 0)
     w_finish(0)
     w_finish(1)
+    for c in range(2, NC - 1):
+        rev_start(c)
+    w_start(2)
+    w_start(3)
     own_local().wait()
     for d in peers:
         own_copy(d).wait_recv()
@@ -291,6 +304,7 @@
         return 0
 
     lax.fori_loop(0, 2, own_step, 0)
+    rev_start(NC - 1)
     w_finish(2)
     w_finish(3)
     w_second(2)
@@ -332,11 +346,9 @@
         return 0
 
     lax.fori_loop(0, NC - 1, edge_step, 0)
-    w_finish(4)
-    w_finish(5)
-    w_second(4)
-    w_second(5)
     edge_step(NC - 1, 0)
+    w_start(4)
+    w_start(5)
 
     def part_wait(c, _):
         part_local(c).wait()
@@ -437,6 +449,10 @@
         return 0
 
     stage(0)
+    w_finish(4)
+    w_finish(5)
+    w_second(4)
+    w_second(5)
     lax.fori_loop(1, last, flow, 0)
     add(last - 1)
     relay_next(2 * last)

time: 75.8 us -> 66.7 us (0.88)
  Pallas kernels: 73.7 us -> 64.6 us
    pallas_call x1, Pallas kernels: 73.7 us -> 64.6 us  [body(): pl.pallas_call(functools.partial(kernel, E, M, cap), name='edge_window',...]
where the time goes in v2:
time: 66.7 us; the launch traced here: 66.5 us
  Pallas kernels  64.6 us (97%)
  local copies, waits for them, and re-layouts  1.87 us (3%)
    pallas_call x1, Pallas kernels, body(): pl.pallas_call(functools.partial(kernel, E, M, cap), name='edge_window',...  64.6 us
    unnamed x1, local copies, waits for them, and re-layouts  1.87 us

profile of v2, /device:TPU:0, one launch (start us, length us, event | category | flops | bytes accessed | tf_op | source)
XLA Modules:
  0.0 66.5 jit_solution(1843995243553324555)
XLA Ops:
  0.0 64.6 %edge_window.1 = bf16[2048,128]{1,0:T(8,128)(2,1)} custom-call(bf16[2048,128]{1,0:T(8,128)(2,1)} %x_in.1, s32[1,2048]{1,0:T(1,128)} %bitcast.4, s32[16,128]{1,0:T(8,128)} %slot_in.1, s32[1,64]{1,0:T(1,128)} %bitcast.6, s32[1,64]{1,0:T(1,128)} %bitcast.7, bf16[512,128]{1,0:T(8,128)(2,1)} %up_e.1, bf16[128,512]{1,0:T(8,128)(2,1)} %down_e.1, ...), custom_call_target="tpu_custom_call" | custom-call | tf_op jit(solution)/shard_map/edge_window/pallas_call | solution.py:540
  64.6 1.9 %copy.14 = bf16[2048,128]{1,0:T(8,128)(2,1)} copy(bf16[2048,128]{1,0:T(8,128)(2,1)} %edge_window.1) | data formatting | bytes 1048576
